TPU v7x, 32 devices: a whole 2x2x4 slice. The times are simulated.
32 devices in a mesh: blk: 2 (over x), head: 4 (over z), weight: 4 (over y, core).
Axes of the slice: x: 2, y: 2, z: 4, core: 2. Of those that a mesh axis runs over, the one named last changes fastest.
Arguments:
- hidden_in: bfloat16 [2048, 2, 768], P(('blk', 'head', 'weight')), may hold values from -6 to 6
- qkv_weight: bfloat16 [768, 2304], replicated, may hold values from -0.21875 to 0.21875
- query_bias: float32 [768], replicated, may hold values from -3 to 3
- value_bias: float32 [768], replicated, may hold values from -0.12 to 0.12
- out_weight: bfloat16 [768, 768], replicated, may hold values from -5.75 to 5.75
- out_bias: float32 [768], replicated, may hold values from -3 to 3
- norm1_gain: float32 [768], replicated, may hold values from 0.25 to 1.75
- norm1_bias: float32 [768], replicated, may hold values from -3 to 3
- up_weight: bfloat16 [768, 3072], P(None, 'weight'), may hold values from -0.21875 to 0.21875
- up_bias: float32 [3072], P('weight'), may hold values from -3 to 3
- down_weight: bfloat16 [3072, 768], P('weight'), may hold values from -0.109375 to 0.109375
- down_bias: float32 [768], replicated, may hold values from -3 to 3
- norm2_gain: float32 [768], replicated, may hold values from 0.25 to 1.75
- norm2_bias: float32 [768], replicated, may hold values from -3 to 3
- lengths: int32 [2], replicated, may hold values from 256 to 2048, as said below
- out_cotangent: bfloat16 [2048, 2, 768], P(('blk', 'head', 'weight')), may hold values from -6 to 6
Outputs:
- layer_out: bfloat16 [2048, 2, 768], P(('blk', 'head', 'weight'))
- grad_in: float32 [2048, 2, 768], P(('blk', 'head', 'weight'))
- grad_qkv_weight: float32 [768, 2304], replicated
- grad_query_bias: float32 [768], replicated
- grad_value_bias: float32 [768], replicated
- grad_out_weight: float32 [768, 768], replicated
- grad_out_bias: float32 [768], replicated
- grad_norm1_gain: float32 [768], replicated
- grad_norm1_bias: float32 [768], replicated
- grad_up_weight: float32 [768, 3072], P(None, 'weight')
- grad_up_bias: float32 [3072], P('weight')
- grad_down_weight: float32 [3072, 768], P('weight')
- grad_down_bias: float32 [768], replicated
- grad_norm2_gain: float32 [768], replicated
- grad_norm2_bias: float32 [768], replicated
Inputs may be any that keep to these rules, and one draw needn't show every extreme that they name: Positions 0 to lengths[b] - 1 of sequence b are tokens and the rest padding; at least one sequence has no padding.
All inputs are finite; a program needn't handle non-finite values.
Results may differ from a plain program's by a relative error of at most 0.02.
Values may be sent and summed in bfloat16 or wider, within the bound.
No kernel may reach another device: no remote copies, remote signals or barrier semaphores. Data moves between devices by JAX's collectives and lax.ppermute only.
A program may use at most 128 MiB of HBM per device.

v0:
```python
import jax
import jax.numpy as jnp
from jax import lax
from jax.sharding import PartitionSpec as P

HEADS = 12
HEAD_DIM = 64


EPS = 1e-05
SQRT_HALF = 0.7071067811865476
INV_ROOT_TAU = 0.3989422804014327


def norm_forward(resid, gain, bias):
    centre = jnp.mean(resid, axis=-1, keepdims=True)
    centred = resid - centre
    spread = jnp.mean(centred * centred, axis=-1, keepdims=True)
    rstd = lax.rsqrt(spread + EPS)
    normed = centred * rstd
    return (normed * gain + bias, normed, rstd)


def norm_backward(grad, normed, rstd, gain):
    scaled = grad * gain
    inner = (
        scaled
        - jnp.mean(scaled, axis=-1, keepdims=True)
        - normed * jnp.mean(scaled * normed, axis=-1, keepdims=True)
    )
    return (rstd * inner, jnp.sum(grad * normed, axis=0), jnp.sum(grad, axis=0))


def gelu_value(pre):
    return 0.5 * pre * (1.0 + jax.scipy.special.erf(pre * SQRT_HALF))


def gelu_slope(pre):
    return (
        0.5 * (1.0 + jax.scipy.special.erf(pre * SQRT_HALF))
        + pre * jnp.exp(-0.5 * pre * pre) * INV_ROOT_TAU
    )


def sweep(step, carry, piece):
    count = jax.tree.leaves(piece)[0].shape[0]
    size = 1024

    def advance(index, state):
        part = jax.tree.map(
            lambda leaf: lax.dynamic_slice_in_dim(leaf, index * size, size, 0), piece
        )
        return step(state, part, index * size)

    return lax.fori_loop(0, count // size, advance, carry)


def per_device(
    hidden_in,
    qkv_weight,
    query_bias,
    value_bias,
    out_weight,
    out_bias,
    norm1_gain,
    norm1_bias,
    up_weight,
    up_bias,
    down_weight,
    down_bias,
    norm2_gain,
    norm2_bias,
    lengths,
    out_cotangent,
):
    rows_here, seq_count, width = hidden_in.shape
    head_devs = lax.axis_size("head")
    weight_devs = lax.axis_size("weight")
    group = width // head_devs
    local_heads = HEADS // head_devs
    scale = HEAD_DIM ** (-0.5)
    tokens = rows_here * seq_count
    flat = hidden_in.reshape(tokens, width)
    bias_all = jnp.concatenate([query_bias, jnp.zeros((width,), jnp.float32), value_bias])
    packed = (jnp.dot(flat, qkv_weight, preferred_element_type=jnp.float32) + bias_all).astype(
        jnp.bfloat16
    )
    packed = packed.reshape(rows_here, seq_count, 3, width)
    regrouped = lax.all_to_all(packed, "head", split_axis=3, concat_axis=0, tiled=True)
    query_rows = regrouped.shape[0]
    query = regrouped[:, :, 0].reshape(query_rows, seq_count, local_heads, HEAD_DIM)
    keyval = regrouped[:, :, 1:]
    key_total = query_rows * lax.axis_size("blk") * weight_devs

    def positions(start, count):
        index = jnp.arange(count, dtype=jnp.int32) + start
        device = index // query_rows
        within = index % query_rows
        source = device // weight_devs * head_devs + within // rows_here
        return (source * weight_devs + device % weight_devs) * rows_here + within % rows_here

    def split_block(block, start):
        count = block.shape[0]
        keys = block[:, :, 0].reshape(count, seq_count, local_heads, HEAD_DIM)
        values = block[:, :, 1].reshape(count, seq_count, local_heads, HEAD_DIM)
        valid = positions(start, count)[None, :] < lengths[:, None]
        scores = (
            jnp.einsum("qbhe,kbhe->bhqk", query, keys, preferred_element_type=jnp.float32) * scale
        )
        weights = jnp.where(valid[:, None, None, :], jnp.exp(scores), 0.0)
        return (keys, values, weights)

    def forward_block(carry, block, start):
        numer, denom = carry
        keys, values, weights = split_block(block, start)
        numer = numer + jnp.einsum(
            "bhqk,kbhe->qbhe",
            weights.astype(jnp.bfloat16),
            values,
            preferred_element_type=jnp.float32,
        )
        return (numer, denom + jnp.sum(weights, axis=-1))

    first = (
        jnp.zeros((query_rows, seq_count, local_heads, HEAD_DIM), jnp.float32),
        jnp.zeros((seq_count, local_heads, query_rows), jnp.float32),
    )
    numer, denom = sweep(
        forward_block, first, lax.all_gather(keyval, ("blk", "weight"), axis=0, tiled=True)
    )
    attended = (numer / jnp.transpose(denom, (2, 0, 1))[..., None]).astype(jnp.bfloat16)
    returned = lax.all_to_all(
        attended.reshape(query_rows, seq_count, group),
        "head",
        split_axis=0,
        concat_axis=2,
        tiled=True,
    )
    attn_flat = returned.reshape(tokens, width)
    resid1 = (
        flat.astype(jnp.float32)
        + jnp.dot(attn_flat, out_weight, preferred_element_type=jnp.float32)
        + out_bias
    )
    hidden1, normed1, rstd1 = norm_forward(resid1, norm1_gain, norm1_bias)
    hidden_half = hidden1.astype(jnp.bfloat16).reshape(rows_here, seq_count, width)
    gathered = lax.all_gather(hidden_half, "weight", axis=0, tiled=True)
    gathered_flat = gathered.reshape(weight_devs * tokens, width)
    pre = jnp.dot(gathered_flat, up_weight, preferred_element_type=jnp.float32) + up_bias
    active = gelu_value(pre).astype(jnp.bfloat16)
    active_rows = active.reshape(weight_devs * rows_here, seq_count, -1)
    count = lax.axis_size("weight") * rows_here
    part = active_rows
    mixed = (
        lax.psum_scatter(
            jnp.dot(
                part.reshape(count * seq_count, -1), down_weight, preferred_element_type=jnp.float32
            )
            .reshape(count, seq_count, width)
            .astype(jnp.bfloat16),
            "weight",
            scatter_dimension=0,
            tiled=True,
        )
        .astype(jnp.float32)
        .reshape(tokens, width)
    )
    resid2 = hidden1 + mixed + down_bias
    final, normed2, rstd2 = norm_forward(resid2, norm2_gain, norm2_bias)
    layer_out = final.astype(jnp.bfloat16).reshape(rows_here, seq_count, width)
    cotangent = out_cotangent.reshape(tokens, width).astype(jnp.float32)
    grad_resid2, grad_norm2_gain, grad_norm2_bias = norm_backward(
        cotangent, normed2, rstd2, norm2_gain
    )
    grad_down_bias = jnp.sum(grad_resid2, axis=0)
    grad_mixed = grad_resid2.astype(jnp.bfloat16).reshape(rows_here, seq_count, width)
    mixed_all = lax.all_gather(grad_mixed, "weight", axis=0, tiled=True).reshape(
        weight_devs * tokens, width
    )
    grad_down_weight = jnp.dot(active.T, mixed_all, preferred_element_type=jnp.float32)
    grad_pre = jnp.dot(mixed_all, down_weight.T, preferred_element_type=jnp.float32) * gelu_slope(
        pre
    )
    grad_up_bias = jnp.sum(grad_pre, axis=0)
    grad_pre_half = grad_pre.astype(jnp.bfloat16)
    grad_up_weight = jnp.dot(gathered_flat.T, grad_pre_half, preferred_element_type=jnp.float32)
    pre_rows = grad_pre_half.reshape(weight_devs * rows_here, seq_count, -1)
    count = lax.axis_size("weight") * rows_here
    part = pre_rows
    back_hidden = (
        lax.psum_scatter(
            jnp.dot(
                part.reshape(count * seq_count, -1), up_weight.T, preferred_element_type=jnp.float32
            )
            .reshape(count, seq_count, width)
            .astype(jnp.bfloat16),
            "weight",
            scatter_dimension=0,
            tiled=True,
        )
        .astype(jnp.float32)
        .reshape(tokens, width)
    )
    grad_hidden1 = grad_resid2 + back_hidden
    grad_resid1, grad_norm1_gain, grad_norm1_bias = norm_backward(
        grad_hidden1, normed1, rstd1, norm1_gain
    )
    grad_out_bias = jnp.sum(grad_resid1, axis=0)
    grad_attn_half = grad_resid1.astype(jnp.bfloat16)
    grad_out_weight = jnp.dot(attn_flat.T, grad_attn_half, preferred_element_type=jnp.float32)
    grad_attended = jnp.dot(
        grad_attn_half, out_weight.T, preferred_element_type=jnp.float32
    ).astype(jnp.bfloat16)
    heads_grad = lax.all_to_all(
        grad_attended.reshape(rows_here, seq_count, width),
        "head",
        split_axis=2,
        concat_axis=0,
        tiled=True,
    )
    heads_grad = heads_grad.reshape(query_rows, seq_count, local_heads, HEAD_DIM)
    delta = jnp.transpose(
        jnp.sum(heads_grad.astype(jnp.float32) * attended.astype(jnp.float32), axis=-1), (1, 2, 0)
    )
    own_start = lax.axis_index(("blk", "weight")) * query_rows
    own_keys = keyval[:, :, 0].reshape(query_rows, seq_count, local_heads, HEAD_DIM)
    own_values = keyval[:, :, 1].reshape(query_rows, seq_count, local_heads, HEAD_DIM)
    own_valid = positions(own_start, query_rows)[None, :] < lengths[:, None]
    delta_rows = jnp.transpose(delta, (2, 0, 1))
    denom_rows = jnp.transpose(denom, (2, 0, 1))

    def key_side(carry, pieces, start):
        key_acc, value_acc, query_sums = carry
        query_piece, grad_piece, delta_piece, denom_piece = pieces
        count = query_piece.shape[0]
        scores = (
            jnp.einsum("qbhe,kbhe->bhqk", query_piece, own_keys, preferred_element_type=jnp.float32)
            * scale
        )
        weights = jnp.where(own_valid[:, None, None, :], jnp.exp(scores), 0.0)
        probs = weights / jnp.transpose(denom_piece, (1, 2, 0))[..., None]
        grad_prob = jnp.einsum(
            "qbhe,kbhe->bhqk", grad_piece, own_values, preferred_element_type=jnp.float32
        )
        score_half = (
            probs * (grad_prob - jnp.transpose(delta_piece, (1, 2, 0))[..., None])
        ).astype(jnp.bfloat16)
        value_acc = value_acc + jnp.einsum(
            "bhqk,qbhe->kbhe",
            probs.astype(jnp.bfloat16),
            grad_piece,
            preferred_element_type=jnp.float32,
        )
        key_acc = (
            key_acc
            + jnp.einsum(
                "bhqk,qbhe->kbhe", score_half, query_piece, preferred_element_type=jnp.float32
            )
            * scale
        )
        query_part = (
            jnp.einsum("bhqk,kbhe->qbhe", score_half, own_keys, preferred_element_type=jnp.float32)
            * scale
        )
        query_sums = lax.dynamic_update_slice_in_dim(
            query_sums, query_part.reshape(count, seq_count, group), start, 0
        )
        return (key_acc, value_acc, query_sums)

    second = (
        jnp.zeros((query_rows, seq_count, local_heads, HEAD_DIM), jnp.float32),
        jnp.zeros((query_rows, seq_count, local_heads, HEAD_DIM), jnp.float32),
        jnp.zeros((key_total, seq_count, group), jnp.float32),
    )
    key_acc, value_acc, query_sums = sweep(
        key_side,
        second,
        (
            lax.all_gather(query, ("blk", "weight"), axis=0, tiled=True),
            lax.all_gather(heads_grad, ("blk", "weight"), axis=0, tiled=True),
            lax.all_gather(
                delta_rows.astype(jnp.bfloat16), ("blk", "weight"), axis=0, tiled=True
            ).astype(jnp.float32),
            lax.all_gather(
                denom_rows.astype(jnp.bfloat16), ("blk", "weight"), axis=0, tiled=True
            ).astype(jnp.float32),
        ),
    )
    query_grad = lax.psum_scatter(
        query_sums.astype(jnp.bfloat16), ("blk", "weight"), scatter_dimension=0, tiled=True
    ).astype(jnp.float32)
    key_grad = key_acc.reshape(query_rows, seq_count, group)
    value_grad = value_acc.reshape(query_rows, seq_count, group)
    stacked = jnp.stack([query_grad, key_grad, value_grad], axis=2).astype(jnp.bfloat16)
    grad_packed = lax.all_to_all(stacked, "head", split_axis=0, concat_axis=3, tiled=True).reshape(
        tokens, 3 * width
    )
    grad_qkv_weight = jnp.dot(flat.T, grad_packed, preferred_element_type=jnp.float32)
    column_sums = jnp.sum(grad_packed.astype(jnp.float32), axis=0)
    grad_in = (
        jnp.dot(grad_packed, qkv_weight.T, preferred_element_type=jnp.float32) + grad_resid1
    ).reshape(rows_here, seq_count, width)
    shared = lax.psum(
        (
            grad_qkv_weight,
            column_sums[:width],
            column_sums[2 * width :],
            grad_out_weight,
            grad_out_bias,
            grad_norm1_gain,
            grad_norm1_bias,
            grad_norm2_gain,
            grad_norm2_bias,
            grad_down_bias,
        ),
        ("blk", "head", "weight"),
    )
    hidden_sums = (
        lax.psum(grad_up_weight.astype(jnp.bfloat16), ("blk", "head")).astype(jnp.float32),
        lax.psum(grad_up_bias.astype(jnp.bfloat16), ("blk", "head")).astype(jnp.float32),
        lax.psum(grad_down_weight.astype(jnp.bfloat16), ("blk", "head")).astype(jnp.float32),
    )
    return (
        layer_out,
        grad_in,
        shared[0],
        shared[1],
        shared[2],
        shared[3],
        shared[4],
        shared[5],
        shared[6],
        hidden_sums[0],
        hidden_sums[1],
        hidden_sums[2],
        shared[9],
        shared[7],
        shared[8],
    )


def solution(mesh):
    placed = (
        P(("blk", "head", "weight"), None, None),
        P(),
        P(),
        P(),
        P(),
        P(),
        P(),
        P(),
        P(None, "weight"),
        P("weight"),
        P("weight", None),
        P(),
        P(),
        P(),
        P(),
        P(("blk", "head", "weight"), None, None),
    )
    return jax.shard_map(
        per_device,
        mesh=mesh,
        in_specs=placed,
        out_specs=(
            P(("blk", "head", "weight"), None, None),
            P(("blk", "head", "weight"), None, None),
            P(),
            P(),
            P(),
            P(),
            P(),
            P(),
            P(),
            P(None, "weight"),
            P("weight"),
            P("weight", None),
            P(),
            P(),
            P(),
        ),
        check_vma=False,
    )
```

profile of v0, /device:TPU:0, one launch (start us, length us, event | category | flops | bytes accessed | tf_op | source)
XLA Modules:
  0.0 749.1 jit_solution(972970801593629136)
XLA Ops:
  21.6 22.3 %all_to_all.63 = bf16[4,2,36864]{2,1,0:T(2,128)(2,1)} all-to-all(bf16[4,2,36864]{2,1,0:T(2,128)(2,1)} %reshape.378), channel_id=1, replica_groups=mesh['blk'=2,'head'=4,'weight'=4] {'head'}, dimensions={0} | all-to-all | bytes 1179648 | tf_op jit(solution)/shard_map/all_to_all | solution.py:89
  46.6 4.8 copy.101
  58.3 32.0 %all-gather.4.cloned.1.call-done = bf16[2048,2,2,192]{3,0,2,1:T(8,128)(2,1)} async-done(((bf16[256,2,2,192]{3,0,2,1:T(8,128)(2,1)}), bf16[2048,2,2,192]{3,0,2,1:T(8,128)(2,1)}) %all-gather.4.cloned.1.call-update) | async-done | bytes 3145744 | tf_op jit(solution)/shard_map/all_gather | solution.py:129
  90.3 6.1 copy.87
  96.4 23.1 %while.37 = (s32[]{:T(128)}, f32[256,2,3,64]{0,3,2,1:T(8,128)}, f32[2,3,256]{2,1,0:T(4,128)S(1)}, bf16[2048,2,2,192]{0,3,1,2:T(8,128)(2,1)}, s32[2]{0:T(128)}, /...) while((s32[]{:T(128)}, f32[256,2,3,64]{0,3,2,1:T(8,128)}, ...), condition=%wide.region_2.3_spmd.clone, body=%wide.region_0.2_spmd.clone.sunk | while | flops 412356096 | bytes 19118340 | solution.py:55
  103.1 4.8 fusion.121
  114.6 4.9 fusion.121
  123.0 13.9 %all_to_all.64 = bf16[256,2,192]{2,1,0:T(2,128)(2,1)S(1)} all-to-all(bf16[256,2,192]{2,1,0:T(2,128)(2,1)} %copy.88), channel_id=1, replica_groups=mesh['blk'=2,'head'=4,'weight'=4] {'head'}, dimensions={0} | all-to-all | bytes 393216 | tf_op jit(solution)/shard_map/all_to_all | solution.py:132
  145.3 9.5 %all_gather.22 = bf16[256,2,768]{2,1,0:T(2,128)(2,1)} all-gather(bf16[64,2,768]{2,1,0:T(2,128)(2,1)} %reshape.355), channel_id=1, replica_groups=mesh['blk'=2,'head'=4,'weight'=4] {'weight'}, dimensions={0}, use_global_device_ids=true | all-gather | bytes 983040 | tf_op jit(solution)/shard_map/all_gather | solution.py:147
  174.6 26.6 %all-reduce.10.cloned.1.call-done = bf16[256,2,768]{2,1,0:T(2,128)(2,1)} async-done(((bf16[256,2,768]{2,1,0:T(2,128)(2,1)}), bf16[256,2,768]{2,1,0:T(2,128)(2,1)}) %all-reduce.10.cloned.1.call-update) | async-done | bytes 786448
  212.0 9.3 %all_gather.25 = bf16[256,2,768]{2,1,0:T(2,128)(2,1)} all-gather(bf16[64,2,768]{2,1,0:T(2,128)(2,1)} %reshape.360), channel_id=1, replica_groups=mesh['blk'=2,'head'=4,'weight'=4] {'weight'}, dimensions={0}, use_global_device_ids=true | all-gather | bytes 983040 | tf_op jit(solution)/shard_map/all_gather | solution.py:177
  234.2 35.0 %all-reduce.12.cloned.1.call-done = bf16[256,2,768]{2,1,0:T(2,128)(2,1)} async-done(((bf16[256,2,768]{2,1,0:T(2,128)(2,1)}), bf16[256,2,768]{2,1,0:T(2,128)(2,1)}) %all-reduce.12.cloned.1.call-update) | async-done | bytes 786448
  284.3 11.5 %all_to_all.65 = bf16[4,2,12288]{2,1,0:T(2,128)(2,1)} all-to-all(bf16[4,2,12288]{2,1,0:T(2,128)(2,1)} %reshape.380), channel_id=1, replica_groups=mesh['blk'=2,'head'=4,'weight'=4] {'head'}, dimensions={0} | all-to-all | bytes 393216 | tf_op jit(solution)/shard_map/all_to_all | solution.py:214
  305.5 8.9 %all_gather.24 = bf16[2048,2,3]{0,2,1:T(4,128)(2,1)S(1)} all-gather(bf16[256,2,3]{0,2,1:T(4,128)(2,1)S(1)} %bitcast_convert_fusion.6), channel_id=1, replica_groups=mesh['blk'=2,'head'=4,'weight'=4] {'blk','weight'}, dimensions={0}, use_global_device_ids=true | all-gather | bytes 27648 | tf_op jit(solution)/shard_map/all_gather | solution.py:284
  316.2 8.6 %all_gather.27 = bf16[2048,2,3]{0,2,1:T(4,128)(2,1)S(1)} all-gather(bf16[256,2,3]{0,2,1:T(4,128)(2,1)S(1)} %multiply_reduce_fusion.2), channel_id=1, replica_groups=mesh['blk'=2,'head'=4,'weight'=4] {'blk','weight'}, dimensions={0}, use_global_device_ids=true | all-gather | bytes 27648 | tf_op jit(solution)/shard_map/all_gather | solution.py:281
  327.4 38.4 %while.38 = (s32[]{:T(128)}, f32[256,2,3,64]{0,3,2,1:T(8,128)}, f32[256,2,3,64]{0,3,2,1:T(8,128)}, bf16[2048,2,192]{0,2,1:T(8,128)(2,1)}, bf16[2048,2,3,64]{0,3,...) while((s32[]{:T(128)}, f32[256,2,3,64]{0,3,2,1:T(8,128)}, ...), condition=%wide.region_15.16_spmd.clone, body=%wide.region_14.15_spmd.clone.sunk | while | flops 1018921472 | bytes 103770656 | solution.py:55
  374.6 29.7 %reduce-scatter.2.cloned.1.call-done = bf16[256,2,192]{0,2,1:T(8,128)(2,1)} async-done(((bf16[2048,2,192]{0,2,1:T(8,128)(2,1)}), bf16[256,2,192]{0,2,1:T(8,128)(2,1)}) %reduce-scatter.2.cloned.1.call-update) | async-done | bytes 196624 | tf_op jit(solution)/shard_map/reduce_scatter | solution.py:289
  416.9 37.5 %all-to-all-done.3 = bf16[256,2,3,192]{3,1,2,0:T(2,128)(2,1)} async-done(((bf16[256,2,3,192]{3,1,2,0:T(2,128)(2,1)}), bf16[256,2,3,192]{3,1,2,0:T(2,128)(2,1)}, u32[]{:S(2)}, u32[]{:S(2)}) %all-to-all-start.3) | async-done | bytes 589856 | tf_op jit(solution)/shard_map/all_to_all | solution.py:295
  460.7 5.2 convolution_bitcast_fusion
  467.6 19.1 %psum.99 = bf16[768]{0:T(1024)(128)(2,1)S(1)} all-reduce(bf16[768]{0:T(1024)(128)(2,1)S(1)} %copy-done.35), channel_id=1, replica_groups=mesh['blk'=2,'head'=4,'weight'=4] {'blk','head'}, use_global_device_ids=true, to_apply=%region_30.31 | all-reduce | flops 768 | bytes 3072 | tf_op jit(solution)/shard_map/psum | solution.py:320
  487.3 45.9 %all-reduce.16.cloned.1.call-done = (bf16[768,768]{1,0:T(8,128)(2,1)}, bf16[768,768]{1,0:T(8,128)(2,1)}) async-done(((bf16[768,768]{1,0:T(8,128)(2,1)}, bf16[768,768]{1,0:T(8,128)(2,1)}), (bf16[768,768]{1,0:T(8,128)(2,1)}, bf16[768,768]{1,0:T(8,128)(2,1)})) %all-reduce.16.cloned.1.call-update) | async-done | bytes 2359312 | tf_op jit(solution)/shard_map/psum | solution.py:319
  546.5 42.4 %all-reduce.2 = (f32[768]{0:T(1024)}, f32[768]{0:T(1024)}, f32[768]{0:T(1024)}, f32[768]{0:T(1024)}, f32[768]{0:T(1024)}, /*index=5*/f32[768]{0:T(1024)}, f32[768]{0:T(1024)}, f32[768]{0:T(1024)}) all-reduce(f32[768]{0:T(1024)} %slice.53, f32[768]{0:T(1024)} %slice.55, ...), channel_id=1, replica_groups=mesh['blk'=2,'head'=4,'weight'=4] {'blk','head','weight'}, use_global_device_ids=true, to_apply=%region_19.20 | all-reduce | flops 6144 | bytes 49152 | tf_op jit(solution)/shard_map/psum | solution.py:303
  588.9 142.2 %all-reduce.14.cloned.1.call-done = (f32[768,2304]{0,1:T(8,128)}, f32[768,768]{1,0:T(8,128)}) async-done(((f32[768,2304]{0,1:T(8,128)}, f32[768,768]{1,0:T(8,128)}), (f32[768,2304]{0,1:T(8,128)}, f32[768,768]{1,0:T(8,128)})) %all-reduce.14.cloned.1.call-update) | async-done | bytes 9437200 | tf_op jit(solution)/shard_map/psum | solution.py:303
  731.1 8.0 %copy.99 = f32[768,2304]{1,0:T(8,128)} copy(f32[768,2304]{0,1:T(8,128)} %get-tuple-element.630) | data formatting | bytes 14155776
  (245 shorter events, 205.5 us)
Async XLA Ops:
  7.2 83.1 %all-gather.4.cloned.1.call-start = ((), (), s32[]{:S(2)}) async-start(), calls=%async_computation.5 | async-start | bytes 4718592 | tf_op jit(solution)/shard_map/all_gather | solution.py:129
  54.4 146.7 %all-reduce.10.cloned.1.call-start = ((), (), s32[]{:S(2)}) async-start(), calls=%async_computation.9 | async-start | bytes 1572864
  136.9 5.9 copy-start.25
  136.9 5.9 copy-start.27
  143.6 14.1 %copy-start.38 = (f32[768]{0:T(1024)S(1)}, f32[768]{0:T(1024)}, u32[]{:S(2)}) copy-start(f32[768]{0:T(1024)} %param.29) | copy-start | bytes 9220
  157.7 4.5 copy-start.36
  163.9 4.9 copy-start.26
  166.8 102.4 %all-reduce.12.cloned.1.call-start = ((), (), s32[]{:S(2)}) async-start(), calls=%async_computation.10 | async-start | bytes 1572864
  224.3 4.7 copy-start.37
  233.6 91.8 %all-gather.6.cloned.1.call-start = ((), (), s32[]{:S(2)}) async-start(), calls=%async_computation.6 | async-start | bytes 1769472 | tf_op jit(solution)/shard_map/all_gather | solution.py:279
  234.1 92.0 %all-gather.8.cloned.1.call-start = ((), (), s32[]{:S(2)}) async-start(), calls=%async_computation.7 | async-start | bytes 1769472 | tf_op jit(solution)/shard_map/all_gather | solution.py:280
  273.0 4.4 copy-start.18
  301.9 102.4 %reduce-scatter.2.cloned.1.call-start = ((), (), s32[]{:S(2)}) async-start(), calls=%async_computation.8 | async-start | bytes 1769472 | tf_op jit(solution)/shard_map/reduce_scatter | solution.py:289
  328.9 3.8 copy-start.12
  340.1 3.8 copy-start.10
  348.1 3.8 copy-start.12
  355.5 3.8 copy-start.5
  359.3 3.8 copy-start.10
  365.9 167.4 %all-reduce.16.cloned.1.call-start = ((), (), s32[]{:S(2)}) async-start(), calls=%async_computation.12 | async-start | bytes 4718592 | tf_op jit(solution)/shard_map/psum | solution.py:319
  409.3 45.2 %all-to-all-start.3 = ((bf16[256,2,3,192]{3,1,2,0:T(2,128)(2,1)}), bf16[256,2,3,192]{3,1,2,0:T(2,128)(2,1)}, u32[]{:S(2)}, u32[]{:S(2)}) async-start(bf16[256,2,3,192]{3,1,2,0:T(2,128)(2,1)} %copy.96), calls=%async_computation.4 | async-start | bytes 1572864 | tf_op jit(solution)/shard_map/all_to_all | solution.py:295
  413.9 317.2 %all-reduce.14.cloned.1.call-start = ((), (), s32[]{:S(2)}) async-start(), calls=%async_computation.11 | async-start | bytes 18874368 | tf_op jit(solution)/shard_map/psum | solution.py:303
  539.8 6.6 copy-start.28
  539.8 6.6 copy-start.29
  539.8 6.6 copy-start.30
  (39 other events, 87.5 us)
Sparse Core Ops, SparseCore 0:
  54.6 35.6 all-gather.3
  166.9 34.1 all-reduce.9
  233.7 35.4 all-reduce.11
  270.9 25.7 all-gather.5
  302.0 24.0 all-gather.7
  366.0 38.2 reduce-scatter.1
  408.4 124.7 all-reduce.15
  539.8 191.2 all-reduce.13
where the time goes:
time: 752 us; the launch traced here: 749 us
  waiting for transfers between devices  350 us (47%)
  blocking collectives  146 us (19%)
  local copies, waits for them, and re-layouts  118 us (16%)
  matrix products  79.5 us (11%)
  other arithmetic  35 us (5%)
  between operations  15.1 us (2%)
    psum x1, waiting for transfers between devices, per_device(): lax.psum((grad_qkv_weight, column_sums[:width], column_sums[2 * width:],...  142 us
    unnamed x10, waiting for transfers between devices  62.2 us
    psum x1, waiting for transfers between devices, per_device(): lax.psum(grad_up_weight.astype(jnp.bfloat16), ('blk', 'head'))  45.9 us
    psum x1, blocking collectives, per_device(): lax.psum((grad_qkv_weight, column_sums[:width], column_sums[2 * width:],...  42.4 us
    all_to_all x1, waiting for transfers between devices, per_device(): lax.all_to_all(stacked, 'head', split_axis=0, concat_axis=3, tiled=True)  37.5 us
    unnamed x68, local copies, waits for them, and re-layouts  34.1 us
    all_gather x1, waiting for transfers between devices, per_device(): lax.all_gather(keyval, ('blk', 'weight'), axis=0, tiled=True)  32 us
    reduce_scatter x1, waiting for transfers between devices, per_device(): lax.psum_scatter(query_sums.astype(jnp.bfloat16), ('blk', 'weight'), scat...  29.7 us
  transfers between devices with their start and end apart: 9, of which 8 were waited for; matrix products, arithmetic and copies ran while one was open for 11% of the time, Pallas kernels for 0%

commit v1 on v0

v1 whole, which is shorter than its diff:
```python
import jax
import jax.numpy as jnp
from jax import lax
from jax.experimental import pallas as pl
from jax.experimental.pallas import tpu as pltpu
from jax.sharding import PartitionSpec as P

HEADS = 12
HEAD_DIM = 64
EPS = 1e-05
SQRT_HALF = 0.7071067811865476
INV_ROOT_TAU = 0.3989422804014327
SCALE = HEAD_DIM ** (-0.5)
FAR = -1e30
F32 = jnp.float32
BF16 = jnp.bfloat16
NT = (((1,), (1,)), ((), ()))
TN = (((0,), (0,)), ((), ()))


def norm_forward(resid, gain, bias):
    centre = jnp.mean(resid, axis=-1, keepdims=True)
    centred = resid - centre
    spread = jnp.mean(centred * centred, axis=-1, keepdims=True)
    rstd = lax.rsqrt(spread + EPS)
    normed = centred * rstd
    return (normed * gain + bias, normed, rstd)


def norm_backward(grad, normed, rstd, gain):
    scaled = grad * gain
    inner = (
        scaled
        - jnp.mean(scaled, axis=-1, keepdims=True)
        - normed * jnp.mean(scaled * normed, axis=-1, keepdims=True)
    )
    return (rstd * inner, jnp.sum(grad * normed, axis=0), jnp.sum(grad, axis=0))


def gelu_value(pre):
    return 0.5 * pre * (1.0 + lax.erf(pre * SQRT_HALF))


def gelu_slope(pre):
    return 0.5 * (1.0 + lax.erf(pre * SQRT_HALF)) + pre * jnp.exp(-0.5 * pre * pre) * INV_ROOT_TAU


def lane_plan(heads):
    data = heads * HEAD_DIM
    wide = -(-(data + 1 + 6 * heads) // 128) * 128
    return data, wide, data + 1, data + 1 + 3 * heads


def head_lanes(heads, head):
    data, wide, delta_at, total_at = lane_plan(heads)
    lane = lax.broadcasted_iota(jnp.int32, (1, wide), 1)

    def within(start, count):
        return (lane >= start) & (lane < start + count)

    own = within(head * HEAD_DIM, HEAD_DIM)
    extra = (
        (lane == data)
        | within(delta_at + 3 * head, 3)
        | within(total_at + 3 * head, 3)
    )
    return own.astype(F32), (own | extra).astype(BF16)


def three_parts(value):
    high = value.astype(BF16).astype(F32)
    rest = value - high
    middle = rest.astype(BF16).astype(F32)
    return high, middle, rest - middle


def spread_parts(values, start, wide):
    lane = lax.broadcasted_iota(jnp.int32, (1, wide), 1)
    out = 0.0
    for head, value in enumerate(values):
        for part, piece in enumerate(three_parts(value)):
            out = out + jnp.where(lane == start + 3 * head + part, piece, 0.0)
    return out


def on_chip(kernel, out_shape, scratch=(), name=None):
    return pl.pallas_call(
        kernel,
        out_shape=out_shape,
        scratch_shapes=list(scratch),
        compiler_params=pltpu.CompilerParams(vmem_limit_bytes=56 * 1024 * 1024),
        name=name,
    )


def attend(packed, packed_all, heads):
    data, wide, _, total_at = lane_plan(heads)
    rows = packed.shape[0]
    keys = packed_all.shape[0]
    block = min(1024, keys)

    def kernel(own_ref, all_ref, out_ref, logs_ref, acc_ref):
        acc_ref[...] = jnp.zeros_like(acc_ref)
        query = own_ref[:, :wide]

        def step(index, _):
            at = pl.ds(pl.multiple_of(index * block, block), block)
            key = all_ref[at, wide : 2 * wide]
            value = all_ref[at, 2 * wide :]
            for head in range(heads):
                _, mask = head_lanes(heads, head)
                scores = lax.dot_general(query * mask, key, NT, preferred_element_type=F32)
                weights = jnp.exp(scores).astype(BF16)
                acc_ref[head] += jnp.dot(weights, value, preferred_element_type=F32)
            return 0

        lax.fori_loop(0, keys // block, step, 0)
        out = jnp.zeros((rows, wide), F32)
        logs = []
        for head in range(heads):
            own, _ = head_lanes(heads, head)
            part = acc_ref[head]
            total = part[:, data : data + 1]
            out = out + (part / total) * own
            logs.append(jnp.log(total))
        out_ref[...] = out.astype(BF16)
        logs_ref[...] = spread_parts(logs, total_at, wide).astype(BF16)

    shape = jax.ShapeDtypeStruct((rows, wide), BF16)
    return on_chip(
        kernel, (shape, shape), [pltpu.VMEM((heads, rows, wide), F32)], name="attend"
    )(packed, packed_all)


def output_grad(grad, out_own, attended, logs, heads):
    data, wide, delta_at, _ = lane_plan(heads)
    rows = grad.shape[0]

    def kernel(grad_ref, weight_ref, att_ref, logs_ref, out_ref):
        back = lax.dot_general(grad_ref[...], weight_ref[...], NT, preferred_element_type=F32)
        back = back.astype(BF16).astype(F32)
        prod = back * att_ref[...].astype(F32)
        deltas = []
        for head in range(heads):
            own, _ = head_lanes(heads, head)
            deltas.append(jnp.sum(prod * own, axis=-1, keepdims=True))
        out = back + spread_parts(deltas, delta_at, wide) + logs_ref[...].astype(F32)
        out_ref[...] = out.astype(BF16)

    return on_chip(kernel, jax.ShapeDtypeStruct((rows, wide), BF16), name="output_grad")(
        grad, out_own, attended, logs
    )


def attend_back(packed, back, packed_all, back_all, heads):
    data, wide, _, total_at = lane_plan(heads)
    rows = packed.shape[0]
    total_rows = packed_all.shape[0]
    block = min(1024, total_rows)

    def kernel(own_ref, back_ref, all_ref, back_all_ref, out_ref, dq_ref, dk_ref, dv_ref):
        dq_ref[...] = jnp.zeros_like(dq_ref)
        dk_ref[...] = jnp.zeros_like(dk_ref)
        dv_ref[...] = jnp.zeros_like(dv_ref)
        lane = lax.broadcasted_iota(jnp.int32, (1, wide), 1)
        logs = ((lane >= total_at) & (lane < total_at + 3 * heads)).astype(BF16)
        back_own = back_ref[...]
        query_own = own_ref[:, :wide] + back_own * logs
        key_own = own_ref[:, wide : 2 * wide]
        value_own = own_ref[:, 2 * wide :]

        def step(index, _):
            at = pl.ds(pl.multiple_of(index * block, block), block)
            key = all_ref[at, wide : 2 * wide]
            value = all_ref[at, 2 * wide :]
            back_in = back_all_ref[at, :]
            query_plain = all_ref[at, :wide]
            query = query_plain + back_in * logs
            for head in range(heads):
                _, mask = head_lanes(heads, head)
                scores = lax.dot_general(query_own * mask, key, NT, preferred_element_type=F32)
                inner = lax.dot_general(back_own * mask, value, NT, preferred_element_type=F32)
                half = (jnp.exp(scores) * inner).astype(BF16)
                dq_ref[head] += jnp.dot(half, key, preferred_element_type=F32)
                scores = lax.dot_general(key_own * mask, query, NT, preferred_element_type=F32)
                probs = jnp.exp(scores)
                inner = lax.dot_general(value_own * mask, back_in, NT, preferred_element_type=F32)
                half = (probs * inner).astype(BF16)
                dv_ref[head] += jnp.dot(probs.astype(BF16), back_in, preferred_element_type=F32)
                dk_ref[head] += jnp.dot(half, query_plain, preferred_element_type=F32)
            return 0

        lax.fori_loop(0, total_rows // block, step, 0)
        for slot, (ref, factor) in enumerate(((dq_ref, SCALE), (dk_ref, 1.0), (dv_ref, 1.0))):
            out = jnp.zeros((rows, wide), F32)
            for head in range(heads):
                own, _ = head_lanes(heads, head)
                out = out + ref[head] * (own * factor)
            out_ref[:, slot * wide : (slot + 1) * wide] = out.astype(BF16)

    acc = pltpu.VMEM((heads, rows, wide), F32)
    return on_chip(
        kernel,
        jax.ShapeDtypeStruct((rows, 3 * wide), BF16),
        [acc, acc, acc],
        name="attend_back",
    )(packed, back, packed_all, back_all)


def bits_of(axis):
    return [(axis, bit) for bit in range(lax.axis_size(axis).bit_length() - 1)]


def bit_value(place):
    axis, bit = place
    return (lax.axis_index(axis) >> bit) & 1


def trade(value, place):
    axis, bit = place
    return lax.ppermute(
        value, axis, [(i, i ^ (1 << bit)) for i in range(lax.axis_size(axis))]
    )


def halve(value, places):
    for place in places:
        half = value.shape[0] // 2
        mine = bit_value(place)
        send = lax.dynamic_slice_in_dim(value, (1 - mine) * half, half, 0).astype(BF16)
        keep = lax.dynamic_slice_in_dim(value, mine * half, half, 0)
        value = keep.astype(F32) + trade(send, place).astype(F32)
    return value


def double(value, place):
    other = trade(value, place)
    first = bit_value(place) == 0
    return jnp.stack([jnp.where(first, value, other), jnp.where(first, other, value)])


def scatter_weight(value):
    for place in bits_of("weight"):
        value = value.reshape((-1, 2) + value.shape[1:])
        mine = bit_value(place)
        send = lax.dynamic_index_in_dim(value, 1 - mine, 1, keepdims=False).astype(BF16)
        keep = lax.dynamic_index_in_dim(value, mine, 1, keepdims=False)
        value = keep + trade(send, place).astype(F32)
    return value[0]


def gather_keys(value):
    out = lax.all_gather(value, "weight", axis=0, tiled=True)
    pairs = lax.axis_size("blk") // 2
    pieces = [out]
    for hop in range(1, pairs):
        perm = [
            (2 * r + s, 2 * ((r + hop) % pairs) + s) for r in range(pairs) for s in range(2)
        ]
        pieces.append(lax.ppermute(out, "blk", perm))
    return out if len(pieces) == 1 else jnp.concatenate(pieces, axis=0)


def per_device(
    hidden_in,
    qkv_weight,
    query_bias,
    value_bias,
    out_weight,
    out_bias,
    norm1_gain,
    norm1_bias,
    up_weight,
    up_bias,
    down_weight,
    down_bias,
    norm2_gain,
    norm2_bias,
    lengths,
    out_cotangent,
):
    rows_here, _, width = hidden_in.shape
    head_devs = lax.axis_size("head")
    weight_devs = lax.axis_size("weight")
    blk = lax.axis_index("blk")
    head_at = lax.axis_index("head")
    weight_at = lax.axis_index("weight")
    seq = blk & 1
    first_seq = seq == 0
    heads = HEADS // head_devs
    data, wide, delta_at, total_at = lane_plan(heads)
    tokens = 2 * rows_here
    swap = ("blk", 0)

    def to_sequence(value):
        zero, one = value[:, 0], value[:, 1]
        mine = jnp.where(first_seq, zero, one)
        other = trade(jnp.where(first_seq, one, zero), swap)
        return jnp.concatenate([mine, other], axis=0)

    def from_sequence(value, narrow):
        mine = value[:rows_here]
        other = trade(value[rows_here:].astype(narrow), swap).astype(value.dtype)
        return jnp.stack(
            [jnp.where(first_seq, mine, other), jnp.where(first_seq, other, mine)], axis=1
        )

    flat = to_sequence(hidden_in)
    cotangent = to_sequence(out_cotangent).astype(F32)

    own = lax.dynamic_slice_in_dim(
        qkv_weight.reshape(width, 3, head_devs, data), head_at, 1, 2
    ).reshape(width, 3, data)
    factor = jnp.array([SCALE, 1.0, 1.0], F32)
    qkv_own = jnp.pad(
        own * factor.astype(BF16)[None, :, None], ((0, 0), (0, 0), (0, wide - data))
    ).reshape(width, 3 * wide)
    extra = jnp.zeros((3, wide), F32)
    extra = extra.at[0, data].set(1.0).at[2, data].set(1.0)
    extra = extra.at[2, delta_at : delta_at + 3 * heads].set(-1.0)
    extra = extra.at[1, total_at : total_at + 3 * heads].set(-1.0)
    bias_own = jnp.stack([
        lax.dynamic_slice_in_dim(query_bias, head_at * data, data) * SCALE,
        jnp.zeros((data,), F32),
        lax.dynamic_slice_in_dim(value_bias, head_at * data, data),
    ])
    bias_own = (jnp.pad(bias_own, ((0, 0), (0, wide - data))) + extra).reshape(1, 3 * wide)
    out_blocks = jnp.pad(
        out_weight.reshape(head_devs, data, width), ((0, 0), (0, wide - data), (0, 0))
    )
    out_own = lax.dynamic_index_in_dim(out_blocks, head_at, 0, keepdims=False)

    rows = lax.all_gather(flat, "head", axis=0, tiled=True)
    index = jnp.arange(head_devs * tokens, dtype=jnp.int32)
    source = index // tokens
    within = index % tokens
    source_blk = blk ^ (within // rows_here)
    position = (
        (source_blk * head_devs + source) * weight_devs + weight_at
    ) * rows_here + within % rows_here
    valid = position < jnp.where(first_seq, lengths[0], lengths[1])
    lane = jnp.arange(3 * wide, dtype=jnp.int32)
    masked = jnp.where((lane == wide + data)[None, :] & ~valid[:, None], FAR, 0.0)
    packed = (
        jnp.dot(rows, qkv_own, preferred_element_type=F32) + bias_own + masked
    ).astype(BF16)
    packed_all = gather_keys(packed)
    attended, logs = attend(packed, packed_all, heads)
    returned = lax.all_to_all(
        attended.reshape(head_devs, tokens, wide), "head", split_axis=0, concat_axis=0
    )
    resid1 = flat.astype(F32) + out_bias
    for group in range(head_devs):
        resid1 = resid1 + jnp.dot(
            returned[group], out_blocks[group], preferred_element_type=F32
        )
    hidden1, normed1, rstd1 = norm_forward(resid1, norm1_gain, norm1_bias)
    gathered = lax.all_gather(hidden1.astype(BF16), "weight", axis=0, tiled=True)
    pre = jnp.dot(gathered, up_weight, preferred_element_type=F32) + up_bias
    active = gelu_value(pre).astype(BF16)
    mixed = scatter_weight(
        jnp.dot(active, down_weight, preferred_element_type=F32).reshape(
            weight_devs, tokens, width
        )
    )
    resid2 = hidden1 + mixed + down_bias
    final, normed2, rstd2 = norm_forward(resid2, norm2_gain, norm2_bias)
    layer_out = from_sequence(final.astype(BF16), BF16)
    grad_resid2, grad_norm2_gain, grad_norm2_bias = norm_backward(
        cotangent, normed2, rstd2, norm2_gain
    )
    grad_down_bias = jnp.sum(grad_resid2, axis=0)
    mixed_all = lax.all_gather(grad_resid2.astype(BF16), "weight", axis=0, tiled=True)
    grad_pre = lax.dot_general(
        mixed_all, down_weight, NT, preferred_element_type=F32
    ) * gelu_slope(pre)
    grad_up_bias = jnp.sum(grad_pre, axis=0)
    grad_pre_half = grad_pre.astype(BF16)
    back_hidden = scatter_weight(
        lax.dot_general(grad_pre_half, up_weight, NT, preferred_element_type=F32).reshape(
            weight_devs, tokens, width
        )
    )
    grad_down_weight = lax.dot_general(active, mixed_all, TN, preferred_element_type=F32)
    grad_up_weight = lax.dot_general(gathered, grad_pre_half, TN, preferred_element_type=F32)
    grad_hidden1 = grad_resid2 + back_hidden
    grad_resid1, grad_norm1_gain, grad_norm1_bias = norm_backward(
        grad_hidden1, normed1, rstd1, norm1_gain
    )
    grad_out_bias = jnp.sum(grad_resid1, axis=0)
    grad_rows = lax.all_gather(grad_resid1.astype(BF16), "head", axis=0, tiled=True)
    back = output_grad(grad_rows, out_own, attended, logs, heads)
    back_all = gather_keys(back)
    grad_packed = attend_back(packed, back, packed_all, back_all, heads)

    grad_qkv_rows = lax.dot_general(grad_packed, rows, TN, preferred_element_type=F32)
    grad_out_rows = lax.dot_general(attended, grad_rows, TN, preferred_element_type=F32)
    stacked = jnp.concatenate(
        [grad_qkv_rows[at * wide : at * wide + data] for at in range(3)]
        + [grad_out_rows[:data]],
        axis=0,
    )
    weight_bits, blk_bits = bits_of("weight"), bits_of("blk")
    places = weight_bits + blk_bits
    piece = halve(stacked, places).astype(BF16)
    gathered_grads = lax.all_gather(piece, "head", axis=0)

    unscaled = jnp.repeat(jnp.array([1.0 / SCALE, 1.0, 1.0], F32), wide).astype(BF16)
    partial = lax.dot_general(
        grad_packed * unscaled, qkv_own, NT, preferred_element_type=F32
    ).astype(BF16)
    partial = lax.all_to_all(
        partial.reshape(head_devs, tokens, width), "head", split_axis=0, concat_axis=0
    )
    grad_in = jnp.sum(partial.astype(F32), axis=0) + grad_resid1
    grad_in = from_sequence(grad_in, BF16)

    column_sums = jnp.sum(grad_packed.astype(F32), axis=0).reshape(3, wide)[:, :data]
    blank = jnp.zeros((2, head_devs, data), F32)
    bias_rows = lax.dynamic_update_slice(
        blank, jnp.stack([column_sums[0], column_sums[2]])[:, None], (0, head_at, 0)
    ).reshape(2, width)
    small = jnp.concatenate(
        [
            bias_rows,
            jnp.stack([
                grad_out_bias,
                grad_norm1_gain,
                grad_norm1_bias,
                grad_norm2_gain,
                grad_norm2_bias,
                grad_down_bias,
            ]),
        ]
    )
    for place in places + bits_of("head"):
        small = small + trade(small, place)

    order = list(range(len(places)))
    half = width // 2

    def fan_out(value, first):
        held = []
        for at in first:
            value = double(value, places[at])
            held.insert(0, at)
        moved = [held.index(at) for at in order]
        count = len(held)
        value = jnp.transpose(value, (count, *moved, count + 1, count + 2))
        return value.reshape(head_devs, -1, half)

    core = order[:1]
    middle = order[1 : len(weight_bits)]
    outer = order[len(weight_bits) :]
    left = fan_out(gathered_grads[:, :, :half], outer + middle + core)
    right = fan_out(gathered_grads[:, :, half:], middle + outer + core)
    full = jnp.concatenate([left, right], axis=2)
    grad_qkv_weight = (
        jnp.transpose(full[:, : 3 * data].reshape(head_devs, 3, data, width), (3, 1, 0, 2))
        .reshape(width, 3 * width)
        .astype(F32)
    )
    grad_out_weight = full[:, 3 * data :].reshape(width, width).astype(F32)
    hidden_sums = lax.psum(
        (grad_up_weight.astype(BF16), grad_down_weight.astype(BF16)), ("blk", "head")
    )
    up_bias_sum = grad_up_bias.reshape(-1, 128)
    for place in blk_bits + bits_of("head"):
        up_bias_sum = up_bias_sum + trade(up_bias_sum, place)
    return (
        layer_out,
        grad_in,
        grad_qkv_weight,
        small[0],
        small[1],
        grad_out_weight,
        small[2],
        small[3],
        small[4],
        hidden_sums[0].astype(F32),
        up_bias_sum.reshape(-1),
        hidden_sums[1].astype(F32),
        small[7],
        small[5],
        small[6],
    )


def solution(mesh):
    placed = (
        P(("blk", "head", "weight"), None, None),
        P(),
        P(),
        P(),
        P(),
        P(),
        P(),
        P(),
        P(None, "weight"),
        P("weight"),
        P("weight", None),
        P(),
        P(),
        P(),
        P(),
        P(("blk", "head", "weight"), None, None),
    )
    return jax.shard_map(
        per_device,
        mesh=mesh,
        in_specs=placed,
        out_specs=(
            P(("blk", "head", "weight"), None, None),
            P(("blk", "head", "weight"), None, None),
            P(),
            P(),
            P(),
            P(),
            P(),
            P(),
            P(),
            P(None, "weight"),
            P("weight"),
            P("weight", None),
            P(),
            P(),
            P(),
        ),
        check_vma=False,
    )
```

time: 752 us -> 375 us (0.50)
  waiting for transfers between devices: 350 us -> 125 us
  local copies, waits for them, and re-layouts: 118 us -> 42 us
  blocking collectives: 146 us -> 78.9 us
  matrix products: 79.5 us -> 18.6 us
  starting transfers between devices: 5.08 us -> 35.3 us
  Pallas kernels: 0 us -> 26.6 us
    psum x2 -> x1, waiting for transfers between devices: 188 us -> 31.2 us  [per_device(): lax.psum((grad_up_weight.astype(BF16), grad_down_weight.astype(BF16)), ('...]
    unnamed x10 -> x3, waiting for transfers between devices: 62.2 us -> 0.05 us
    psum x2 -> x0, blocking collectives: 61.5 us -> none  [the longest x1 42.4 us: per_device(): lax.psum((grad_qkv_weight, column_sums[:width], column_sums[2 * width:],...]
    dot_general x26 -> x14, matrix products: 79.5 us -> 18.6 us  [the longest x1 3.21 us: per_device(): lax.dot_general(active, mixed_all, TN, preferred_element_type=F32)]
    all_to_all x3 -> x0, blocking collectives: 47.7 us -> none  [the longest x1 22.3 us: per_device(): lax.all_to_all(packed, 'head', split_axis=3, concat_axis=0, tiled=True)]
    ppermute x0 -> x25, waiting for transfers between devices: none -> 43.2 us  [trade(): lax.ppermute(value, axis, [(i, i ^ 1 << bit) for i in range(lax.axis_size...]
    all_gather x4 -> x5, blocking collectives: 36.3 us -> 78.9 us  [the longest x1 24.1 us: per_device(): gathered_grads = lax.all_gather(piece, 'head', axis=0)]
    reshape x17 -> x2, local copies, waits for them, and re-layouts: 37.6 us -> 0.1 us  [the longest x1 0.09 us: per_device(): bias_rows = lax.dynamic_update_slice(blank, jnp.stack([column_sums[0], co...]
  transfers between devices with their start and end apart: 9 -> 30, of which waited for: 8 -> 16; matrix products, arithmetic and copies ran while one was open for 11% -> 13% of each run, Pallas kernels for 0% -> 0%
where the time goes in v1:
time: 375 us; the launch traced here: 374 us
  waiting for transfers between devices  125 us (33%)
  blocking collectives  78.9 us (21%)
  local copies, waits for them, and re-layouts  42 us (11%)
  starting transfers between devices  35.3 us (9%)
  other arithmetic  31 us (8%)
  Pallas kernels  26.6 us (7%)
  matrix products  18.6 us (5%)
  between operations  16.5 us (4%)
    ppermute x25, waiting for transfers between devices, trade(): lax.ppermute(value, axis, [(i, i ^ 1 << bit) for i in range(lax.axis_size...  43.2 us
    all_gather x2, waiting for transfers between devices, gather_keys(): out = lax.all_gather(value, 'weight', axis=0, tiled=True)  41 us
    psum x1, waiting for transfers between devices, per_device(): lax.psum((grad_up_weight.astype(BF16), grad_down_weight.astype(BF16)), ('...  31.2 us
    ppermute x25, starting transfers between devices, trade(): lax.ppermute(value, axis, [(i, i ^ 1 << bit) for i in range(lax.axis_size...  27.2 us
    all_gather x1, blocking collectives, per_device(): gathered_grads = lax.all_gather(piece, 'head', axis=0)  24.1 us
    unnamed x102, local copies, waits for them, and re-layouts  21.6 us
    all_gather x1, blocking collectives, per_device(): rows = lax.all_gather(flat, 'head', axis=0, tiled=True)  19.8 us
    all_gather x1, blocking collectives, per_device(): lax.all_gather(grad_resid1.astype(BF16), 'head', axis=0, tiled=True)  18.5 us
  transfers between devices with their start and end apart: 30, of which 16 were waited for; matrix products, arithmetic and copies ran while one was open for 13% of the time, Pallas kernels for 0%

profile of v1, /device:TPU:0, one launch (start us, length us, event | category | flops | bytes accessed | tf_op | source)
XLA Modules:
  0.0 373.7 jit_solution(354533118165695941)
XLA Ops:
  19.5 5.8 %copy.42 = bf16[768,2304]{0,1:T(8,128)(2,1)} copy(bf16[768,2304]{1,0:T(8,128)(2,1)} %param.27) | data formatting | bytes 7077888 | tf_op args[1]
  28.0 19.8 %all_gather.24 = bf16[512,768]{1,0:T(8,128)(2,1)S(1)} all-gather(bf16[128,768]{1,0:T(8,128)(2,1)S(1)} %pad_maximum_fusion.8), channel_id=1, replica_groups=mesh['blk'=2,'head'=4,'weight'=4] {'head'}, dimensions={0}, use_global_device_ids=true | all-gather | bytes 983040 | tf_op jit(solution)/shard_map/all_gather | solution.py:333
  49.6 27.0 %all-gather.4.cloned.1.call-done.all_ref = bf16[2048,768]{1,0:T(8,128)(2,1)} async-done(((bf16[512,768]{1,0:T(8,128)(2,1)}), bf16[2048,768]{1,0:T(8,128)(2,1)}) %all-gather.4.cloned.1.call-update) | async-done | bytes 3145744 | tf_op jit(solution)/shard_map/all_gather | solution.py:253
  76.7 7.6 %attend.1 = (bf16[512,256]{1,0:T(8,128)(2,1)}, bf16[512,256]{1,0:T(8,128)(2,1)}) custom-call(bf16[512,768]{1,0:T(8,128)(2,1)} %add_convert_fusion.own_ref, bf16[2048,768]{1,0:T(8,128)(2,1)} %all-gather.4.cloned.1.call-done.all_ref), custom_call_target="tpu_custom_call" | custom-call | tf_op jit(solution)/shard_map/attend/pallas_call | solution.py:130
  84.3 4.6 %all-to-all-start = ((bf16[4,128,256]{2,1,0:T(8,128)(2,1)}), bf16[4,128,256]{2,1,0:T(8,128)(2,1)S(1)}, u32[]{:S(2)}, u32[]{:S(2)}) async-start(bf16[4,128,256]{2,1,0:T(8,128)(2,1)} %bitcast.170), calls=%async_computation | async-start | bytes 524288 | tf_op jit(solution)/shard_map/all_to_all | solution.py:349
  88.9 9.3 %all-to-all-done = bf16[4,128,256]{2,1,0:T(8,128)(2,1)S(1)} async-done(((bf16[4,128,256]{2,1,0:T(8,128)(2,1)}), bf16[4,128,256]{2,1,0:T(8,128)(2,1)S(1)}, u32[]{:S(2)}, u32[]{:S(2)}) %all-to-all-start) | async-done | bytes 262176 | tf_op jit(solution)/shard_map/all_to_all | solution.py:349
  101.4 7.7 %all_gather.26 = bf16[512,768]{1,0:T(8,128)(2,1)S(1)} all-gather(bf16[128,768]{1,0:T(8,128)(2,1)S(1)} %fusion.32), channel_id=1, replica_groups=mesh['blk'=2,'head'=4,'weight'=4] {'weight'}, dimensions={0}, use_global_device_ids=true | all-gather | bytes 983040 | tf_op jit(solution)/shard_map/all_gather | solution.py:358
  122.5 3.8 %collective-permute-done.2 = bf16[1,128,768]{2,1,0:T(8,128)(2,1)} collective-permute-done((bf16[1,128,768]{2,1,0:T(8,128)(2,1)}, bf16[1,128,768]{2,1,0:T(8,128)(2,1)}, u32[]{:S(2)}, u32[]{:S(2)}) %collective-permute-start.2) | collective-permute-done | bytes 196640 | tf_op jit(solution)/shard_map/ppermute | solution.py:221
  132.2 8.8 %all_gather.27 = bf16[512,768]{1,0:T(8,128)(2,1)S(1)} all-gather(bf16[128,768]{1,0:T(8,128)(2,1)S(1)} %convert_element_type.157), channel_id=1, replica_groups=mesh['blk'=2,'head'=4,'weight'=4] {'weight'}, dimensions={0}, use_global_device_ids=true | all-gather | bytes 983040 | tf_op jit(solution)/shard_map/all_gather | solution.py:373
  147.1 5.6 %collective-permute-done.6 = bf16[1,128,768]{2,1,0:T(8,128)(2,1)S(1)} collective-permute-done((bf16[1,128,768]{2,1,0:T(8,128)(2,1)S(1)}, bf16[1,128,768]{2,1,0:T(8,128)(2,1)S(1)}, u32[]{:S(2)}, u32[]{:S(2)}) %collective-permute-start.6) | collective-permute-done | bytes 196640 | tf_op jit(solution)/shard_map/ppermute | solution.py:221
  154.6 18.5 %all_gather.28.grad_ref = bf16[512,768]{1,0:T(8,128)(2,1)} all-gather(bf16[128,768]{1,0:T(8,128)(2,1)S(1)} %convert_element_type.164), channel_id=1, replica_groups=mesh['blk'=2,'head'=4,'weight'=4] {'head'}, dimensions={0}, use_global_device_ids=true | all-gather | bytes 983040 | tf_op jit(solution)/shard_map/all_gather | solution.py:391
  177.3 14.0 %all-gather.6.cloned.1.call-done.back_all_ref = bf16[2048,256]{1,0:T(8,128)(2,1)} async-done(((bf16[512,256]{1,0:T(8,128)(2,1)}), bf16[2048,256]{1,0:T(8,128)(2,1)}) %all-gather.6.cloned.1.call-update) | async-done | bytes 1048592 | tf_op jit(solution)/shard_map/all_gather | solution.py:253
  191.2 16.1 %attend_back.1 = bf16[512,768]{1,0:T(8,128)(2,1)} custom-call(bf16[512,768]{1,0:T(8,128)(2,1)} %add_convert_fusion.own_ref, bf16[512,256]{1,0:T(8,128)(2,1)} %output_grad.1.back_ref, bf16[2048,768]{1,0:T(8,128)(2,1)} %all-gather.4.cloned.1.call-done.all_ref, bf16[2048,256]{1,0:T(8,128)(2,1)} %all-gather.6.cloned.1.call-done.back_all_ref), custom_call_target="tpu_custom_call" | custom-call | tf_op jit(solution)/shard_map/attend_back/pallas_call | solution.py:202
  226.4 6.5 %collective-permute-done.9 = bf16[192,768]{1,0:T(8,128)(2,1)S(1)} collective-permute-done((bf16[192,768]{1,0:T(8,128)(2,1)S(1)}, bf16[192,768]{1,0:T(8,128)(2,1)S(1)}, u32[]{:S(2)}, u32[]{:S(2)}) %collective-permute-start.9) | collective-permute-done | bytes 294944 | tf_op jit(solution)/shard_map/ppermute | solution.py:221
  235.4 5.4 %collective-permute-done.10 = bf16[96,768]{1,0:T(8,128)(2,1)S(1)} collective-permute-done((bf16[96,768]{1,0:T(8,128)(2,1)S(1)}, bf16[96,768]{1,0:T(8,128)(2,1)S(1)}, u32[]{:S(2)}, u32[]{:S(2)}) %collective-permute-start.10) | collective-permute-done | bytes 147488 | tf_op jit(solution)/shard_map/ppermute | solution.py:221
  240.8 24.1 %all-gather = bf16[384,768]{1,0:T(8,128)(2,1)S(1)} all-gather(bf16[96,768]{1,0:T(8,128)(2,1)S(1)} %add_convert_fusion.2), channel_id=2, replica_groups=mesh['blk'=2,'head'=4,'weight'=4] {'head'}, dimensions={0}, use_global_device_ids=true | all-gather | bytes 737280 | tf_op jit(solution)/shard_map/all_gather | solution.py:406
  272.8 3.9 %collective-permute-done.11 = bf16[4,96,384]{2,1,0:T(8,128)(2,1)S(1)} collective-permute-done((bf16[4,96,384]{2,1,0:T(8,128)(2,1)S(1)}, bf16[4,96,384]{2,1,0:T(8,128)(2,1)S(1)}, u32[]{:S(2)}, u32[]{:S(2)}) %collective-permute-start.11) | collective-permute-done | bytes 294944 | tf_op jit(solution)/shard_map/ppermute | solution.py:221
  282.2 3.5 all-to-all-start.1
  285.7 5.5 %collective-permute-done.19 = f32[8,768]{1,0:T(8,128)S(1)} collective-permute-done((f32[8,768]{1,0:T(8,128)S(1)}, f32[8,768]{1,0:T(8,128)S(1)}, u32[]{:S(2)}, u32[]{:S(2)}) %collective-permute-start.19) | collective-permute-done | bytes 24608 | tf_op jit(solution)/shard_map/ppermute | solution.py:221
  298.2 3.8 %collective-permute-start.21 = (f32[8,768]{1,0:T(8,128)S(1)}, f32[8,768]{1,0:T(8,128)S(1)}, u32[]{:S(2)}, u32[]{:S(2)}) collective-permute-start(f32[8,768]{1,0:T(8,128)S(1)} %add.319), channel_id=1, source_target_pairs={{0,8},{4,12},{8,0},{12,4},{1,9},{5,13},{9,1},{13,5},{2,10},{6,14},... | collective-permute-start | bytes 73736 | tf_op jit(solution)/shard_map/ppermute | solution.py:221
  302.0 3.4 collective-permute-done.12
  312.4 31.2 %all-reduce.6.cloned.1.call-done = (bf16[768,768]{1,0:T(8,128)(2,1)}, bf16[768,768]{1,0:T(8,128)(2,1)}) async-done(((bf16[768,768]{1,0:T(8,128)(2,1)}, bf16[768,768]{1,0:T(8,128)(2,1)}), (bf16[768,768]{1,0:T(8,128)(2,1)}, bf16[768,768]{1,0:T(8,128)(2,1)})) %all-reduce.6.cloned.1.call-update) | async-done | bytes 2359312 | tf_op jit(solution)/shard_map/psum | solution.py:464
  355.5 3.6 copy.53
  359.1 8.1 %copy.56 = f32[768,2304]{1,0:T(8,128)} copy(f32[768,2304]{0,1:T(8,128)} %bitcast.161) | data formatting | bytes 14155776
  (274 shorter events, 109.5 us)
Async XLA Ops:
  7.2 69.5 %all-gather.4.cloned.1.call-start = ((), (), s32[]{:S(2)}) async-start(), calls=%async_computation.2 | async-start | bytes 3932160 | tf_op jit(solution)/shard_map/all_gather | solution.py:253
  8.8 19.2 %collective-permute-start = (bf16[64,768]{1,0:T(8,128)(2,1)S(1)}, bf16[64,768]{1,0:T(8,128)(2,1)S(1)}, u32[]{:S(2)}, u32[]{:S(2)}) collective-permute-start(bf16[64,768]{1,0:T(8,128)(2,1)S(1)} %get-tuple-element.147), channel_id=1, source_target_pairs={{0,16},{16,0},{1,17},{17,1},{2,18},{18,2},{3,19},{19,3},{4,20},{20... | collective-permute-start | bytes 294920 | tf_op jit(solution)/shard_map/ppermute | solution.py:221
  84.3 13.9 %all-to-all-start = ((bf16[4,128,256]{2,1,0:T(8,128)(2,1)}), bf16[4,128,256]{2,1,0:T(8,128)(2,1)S(1)}, u32[]{:S(2)}, u32[]{:S(2)}) async-start(bf16[4,128,256]{2,1,0:T(8,128)(2,1)} %bitcast.170), calls=%async_computation | async-start | bytes 524288 | tf_op jit(solution)/shard_map/all_to_all | solution.py:349
  88.9 102.3 %all-gather.6.cloned.1.call-start = ((), (), s32[]{:S(2)}) async-start(), calls=%async_computation.3 | async-start | bytes 1310720 | tf_op jit(solution)/shard_map/all_gather | solution.py:253
  118.8 7.5 %collective-permute-start.2 = (bf16[1,128,768]{2,1,0:T(8,128)(2,1)}, bf16[1,128,768]{2,1,0:T(8,128)(2,1)}, u32[]{:S(2)}, u32[]{:S(2)}) collective-permute-start(bf16[1,128,768]{2,1,0:T(8,128)(2,1)} %dynamic-slice_convert_fusion.3), channel_id=1, source_target_pairs={{0,2},{1,3},{2,0},{3,1},{4,6},{5,7},{6,4},{7,5},{8,10},{9,11},{10,... | collective-permute-start | bytes 589832 | tf_op jit(solution)/shard_map/ppermute | solution.py:221
  145.5 7.2 %collective-permute-start.6 = (bf16[1,128,768]{2,1,0:T(8,128)(2,1)S(1)}, bf16[1,128,768]{2,1,0:T(8,128)(2,1)S(1)}, u32[]{:S(2)}, u32[]{:S(2)}) collective-permute-start(bf16[1,128,768]{2,1,0:T(8,128)(2,1)S(1)} %dynamic-slice_convert_fusion.2), channel_id=1, source_target_pairs={{0,2},{1,3},{2,0},{3,1},{4,6},{5,7},{6,4},{7,5},{8,10},{9,11},{10,... | collective-permute-start | bytes 589832 | tf_op jit(solution)/shard_map/ppermute | solution.py:221
  176.0 167.6 %all-reduce.6.cloned.1.call-start = ((), (), s32[]{:S(2)}) async-start(), calls=%async_computation.4 | async-start | bytes 4718592 | tf_op jit(solution)/shard_map/psum | solution.py:464
  211.4 10.3 %collective-permute-start.8 = (bf16[384,768]{1,0:T(8,128)(2,1)}, bf16[384,768]{1,0:T(8,128)(2,1)}, u32[]{:S(2)}, u32[]{:S(2)}) collective-permute-start(bf16[384,768]{1,0:T(8,128)(2,1)} %dynamic-slice_convert_fusion), channel_id=1, source_target_pairs={{0,1},{1,0},{2,3},{3,2},{4,5},{5,4},{6,7},{7,6},{8,9},{9,8},{10,11... | collective-permute-start | bytes 1769480 | tf_op jit(solution)/shard_map/ppermute | solution.py:221
  214.6 80.2 %collective-permute-start.3 = (bf16[64,768]{1,0:T(8,128)(2,1)}, bf16[64,768]{1,0:T(8,128)(2,1)}, u32[]{:S(2)}, u32[]{:S(2)}) collective-permute-start(bf16[64,768]{1,0:T(8,128)(2,1)} %slice.235), channel_id=1, source_target_pairs={{0,16},{16,0},{1,17},{17,1},{2,18},{18,2},{3,19},{19,3},{4,20},{20... | collective-permute-start | bytes 294920 | tf_op jit(solution)/shard_map/ppermute | solution.py:221
  216.0 8.5 %collective-permute-start.22 = (f32[6,128]{1,0:T(8,128)}, f32[6,128]{1,0:T(8,128)S(1)}, u32[]{:S(2)}, u32[]{:S(2)}) collective-permute-start(f32[6,128]{1,0:T(8,128)} %bitcast.178), channel_id=1, source_target_pairs={{0,16},{16,0},{1,17},{17,1},{2,18},{18,2},{3,19},{19,3},{4,20},{20... | collective-permute-start | bytes 9224 | tf_op jit(solution)/shard_map/ppermute | solution.py:221
  224.0 8.8 %collective-permute-start.9 = (bf16[192,768]{1,0:T(8,128)(2,1)S(1)}, bf16[192,768]{1,0:T(8,128)(2,1)S(1)}, u32[]{:S(2)}, u32[]{:S(2)}) collective-permute-start(bf16[192,768]{1,0:T(8,128)(2,1)S(1)} %dynamic-slice_convert_fusion.1), channel_id=1, source_target_pairs={{0,2},{1,3},{2,0},{3,1},{4,6},{5,7},{6,4},{7,5},{8,10},{9,11},{10,... | collective-permute-start | bytes 884744 | tf_op jit(solution)/shard_map/ppermute | solution.py:221
  224.6 43.2 %collective-permute-start.23 = (f32[6,128]{1,0:T(8,128)S(1)}, f32[6,128]{1,0:T(8,128)S(1)}, u32[]{:S(2)}, u32[]{:S(2)}) collective-permute-start(f32[6,128]{1,0:T(8,128)S(1)} %bitcast_add_fusion.4), channel_id=1, source_target_pairs={{0,4},{4,0},{8,12},{12,8},{1,5},{5,1},{9,13},{13,9},{2,6},{6,2},{1... | collective-permute-start | bytes 9224 | tf_op jit(solution)/shard_map/ppermute | solution.py:221
  265.0 7.8 %collective-permute-start.14 = (bf16[4,96,384]{2,1,0:T(8,128)(2,1)S(1)}, bf16[4,96,384]{2,1,0:T(8,128)(2,1)S(1)}, u32[]{:S(2)}, u32[]{:S(2)}) collective-permute-start(bf16[4,96,384]{2,1,0:T(8,128)(2,1)S(1)} %get-tuple-element.139), channel_id=1, source_target_pairs={{0,2},{1,3},{2,0},{3,1},{4,6},{5,7},{6,4},{7,5},{8,10},{9,11},{10,... | collective-permute-start | bytes 884744 | tf_op jit(solution)/shard_map/ppermute | solution.py:221
  266.7 10.1 %collective-permute-start.11 = (bf16[4,96,384]{2,1,0:T(8,128)(2,1)S(1)}, bf16[4,96,384]{2,1,0:T(8,128)(2,1)S(1)}, u32[]{:S(2)}, u32[]{:S(2)}) collective-permute-start(bf16[4,96,384]{2,1,0:T(8,128)(2,1)S(1)} %get-tuple-element.140), channel_id=1, source_target_pairs={{0,16},{16,0},{1,17},{17,1},{2,18},{18,2},{3,19},{19,3},{4,20},{20... | collective-permute-start | bytes 884744 | tf_op jit(solution)/shard_map/ppermute | solution.py:221
  267.7 11.3 %collective-permute-start.24 = (f32[6,128]{1,0:T(8,128)S(1)}, f32[6,128]{1,0:T(8,128)S(1)}, u32[]{:S(2)}, u32[]{:S(2)}) collective-permute-start(f32[6,128]{1,0:T(8,128)S(1)} %fusion.91), channel_id=1, source_target_pairs={{0,8},{4,12},{8,0},{12,4},{1,9},{5,13},{9,1},{13,5},{2,10},{6,14},... | collective-permute-start | bytes 9224 | tf_op jit(solution)/shard_map/ppermute | solution.py:221
  269.0 10.7 %collective-permute-start.18 = (f32[8,768]{1,0:T(8,128)S(1)}, f32[8,768]{1,0:T(8,128)S(1)}, u32[]{:S(2)}, u32[]{:S(2)}) collective-permute-start(f32[8,768]{1,0:T(8,128)S(1)} %add.316), channel_id=1, source_target_pairs={{0,2},{1,3},{2,0},{3,1},{4,6},{5,7},{6,4},{7,5},{8,10},{9,11},{10,... | collective-permute-start | bytes 73736 | tf_op jit(solution)/shard_map/ppermute | solution.py:221
  277.8 15.7 %collective-permute-start.15 = (bf16[2,4,96,384]{3,2,0,1:T(8,128)(2,1)}, bf16[2,4,96,384]{3,2,0,1:T(8,128)(2,1)S(1)}, u32[]{:S(2)}, u32[]{:S(2)}) collective-permute-start(bf16[2,4,96,384]{3,2,0,1:T(8,128)(2,1)} %pad_maximum_fusion.6), channel_id=1, source_target_pairs={{0,16},{16,0},{1,17},{17,1},{2,18},{18,2},{3,19},{19,3},{4,20},{20... | collective-permute-start | bytes 1769480 | tf_op jit(solution)/shard_map/ppermute | solution.py:221
  279.7 11.5 %collective-permute-start.19 = (f32[8,768]{1,0:T(8,128)S(1)}, f32[8,768]{1,0:T(8,128)S(1)}, u32[]{:S(2)}, u32[]{:S(2)}) collective-permute-start(f32[8,768]{1,0:T(8,128)S(1)} %add.317), channel_id=1, source_target_pairs={{0,16},{16,0},{1,17},{17,1},{2,18},{18,2},{3,19},{19,3},{4,20},{20... | collective-permute-start | bytes 73736 | tf_op jit(solution)/shard_map/ppermute | solution.py:221
  282.2 27.8 %all-to-all-start.1 = ((bf16[4,128,768]{2,1,0:T(8,128)(2,1)}), bf16[4,128,768]{2,1,0:T(8,128)(2,1)S(1)}, u32[]{:S(2)}, u32[]{:S(2)}) async-start(bf16[4,128,768]{2,1,0:T(8,128)(2,1)} %bitcast.177), calls=%async_computation.1 | async-start | bytes 1572864 | tf_op jit(solution)/shard_map/all_to_all | solution.py:412
  292.8 12.6 %collective-permute-start.12 = (bf16[2,4,96,384]{3,2,1,0:T(8,128)(2,1)S(1)}, bf16[2,4,96,384]{3,2,1,0:T(8,128)(2,1)S(1)}, u32[]{:S(2)}, u32[]{:S(2)}) collective-permute-start(bf16[2,4,96,384]{3,2,1,0:T(8,128)(2,1)S(1)} %pad_maximum_fusion.5), channel_id=1, source_target_pairs={{0,2},{1,3},{2,0},{3,1},{4,6},{5,7},{6,4},{7,5},{8,10},{9,11},{10,... | collective-permute-start | bytes 1769480 | tf_op jit(solution)/shard_map/ppermute | solution.py:221
  294.8 54.5 %collective-permute-start.16 = (bf16[2,2,4,96,384]{4,3,1,0,2:T(8,128)(2,1)}, bf16[2,2,4,96,384]{4,3,1,0,2:T(8,128)(2,1)}, u32[]{:S(2)}, u32[]{:S(2)}) collective-permute-start(bf16[2,2,4,96,384]{4,3,1,0,2:T(8,128)(2,1)} %pad_maximum_fusion.4), channel_id=1, source_target_pairs={{0,1},{1,0},{2,3},{3,2},{4,5},{5,4},{6,7},{7,6},{8,9},{9,8},{10,11... | collective-permute-start | bytes 3538952 | tf_op jit(solution)/shard_map/ppermute | solution.py:221
  298.2 11.2 %collective-permute-start.21 = (f32[8,768]{1,0:T(8,128)S(1)}, f32[8,768]{1,0:T(8,128)S(1)}, u32[]{:S(2)}, u32[]{:S(2)}) collective-permute-start(f32[8,768]{1,0:T(8,128)S(1)} %add.319), channel_id=1, source_target_pairs={{0,8},{4,12},{8,0},{12,4},{1,9},{5,13},{9,1},{13,5},{2,10},{6,14},... | collective-permute-start | bytes 73736 | tf_op jit(solution)/shard_map/ppermute | solution.py:221
  306.9 44.6 %collective-permute-start.13 = (bf16[2,2,4,96,384]{4,3,1,0,2:T(8,128)(2,1)}, bf16[2,2,4,96,384]{4,3,1,0,2:T(8,128)(2,1)}, u32[]{:S(2)}, u32[]{:S(2)}) collective-permute-start(bf16[2,2,4,96,384]{4,3,1,0,2:T(8,128)(2,1)} %copy.57), channel_id=1, source_target_pairs={{0,1},{1,0},{2,3},{3,2},{4,5},{5,4},{6,7},{7,6},{8,9},{9,8},{10,11... | collective-permute-start | bytes 3538952 | tf_op jit(solution)/shard_map/ppermute | solution.py:221
  310.1 38.0 %collective-permute-start.7 = (bf16[64,768]{1,0:T(8,128)(2,1)S(1)}, bf16[64,768]{1,0:T(8,128)(2,1)S(1)}, u32[]{:S(2)}, u32[]{:S(2)}) collective-permute-start(bf16[64,768]{1,0:T(8,128)(2,1)S(1)} %slice.304), channel_id=1, source_target_pairs={{0,16},{16,0},{1,17},{17,1},{2,18},{18,2},{3,19},{19,3},{4,20},{20... | collective-permute-start | bytes 294920 | tf_op jit(solution)/shard_map/ppermute | solution.py:221
  (55 other events, 477.6 us)
Sparse Core Ops, SparseCore 0:
  49.7 26.8 all-gather.3
  176.2 15.0 all-gather.5
  221.8 121.7 all-reduce.5
